TPU v7x, 256 devices: a whole 4x4x8 slice. The times are simulated.
256 devices in a mesh: frames: 32 (over z_hi, y, x), rows: 2 (over core), batch: 4 (over z_lo).
Axes of the slice: x: 4, y: 4, z: 8 (z_hi: 2, z_lo: 4; z = z_hi * 4 + z_lo), core: 2. Of those that a mesh axis runs over, the one named last changes fastest.
Arguments:
- video: bfloat16 [256, 32, 128, 320], P(('batch', 'frames'), 'rows'), parts along dimension 0, may hold values from -6 to 6
- w_spatial: bfloat16 [3, 3, 320, 320], replicated, may hold values from -0.109375 to 0.109375
- b_spatial: float32 [320], replicated, may hold values from -3 to 3
- w_temporal: bfloat16 [3, 320, 320], replicated, may hold values from -0.1875 to 0.1875
- b_temporal: float32 [320], replicated, may hold values from -3 to 3
Outputs:
- downsampled: bfloat16 [128, 32, 128, 320], P(('batch', 'frames'), 'rows'), parts along dimension 0
There are 4 independent parts, one for each index of `batch`. A program takes and returns all parts, laid end to end along the dimension named above; an argument that names none is the same for every part. Nothing has to cross between parts.
All inputs are finite; a program needn't handle non-finite values.
Results may differ from a plain program's by a relative error of at most 0.0042.
Values may be sent and summed in bfloat16 or wider, within the bound.
A program may use at most 64 MiB of HBM per device.

v0:
```python
import jax
import jax.numpy as jnp
from jax import lax
from jax.sharding import PartitionSpec as P


def with_halo(cells, sides, width):
    for axis, dim in sides:
        count = lax.axis_size(axis)
        ends = count - 1
        head = lax.slice_in_dim(cells, 0, width, axis=dim)
        tail = lax.slice_in_dim(cells, cells.shape[dim] - width, cells.shape[dim], axis=dim)
        cells = jnp.concatenate(
            [
                lax.ppermute(tail, axis, [(i, (i + 1) % count) for i in range(ends)]),
                cells,
                lax.ppermute(head, axis, [((i + 1) % count, i) for i in range(ends)]),
            ],
            axis=dim,
        )
    return cells


def shifted(block, axis, distance):
    devices = range(lax.axis_size(axis))
    route = [(i - distance, i) for i in devices if i - distance in devices]
    return lax.ppermute(block, axis, route)


def temporal_mix(prev_frames, even_frames, odd_frames, w_temporal, b_temporal):
    total = jnp.dot(prev_frames, w_temporal[0], preferred_element_type=jnp.float32)
    total = total + jnp.dot(even_frames, w_temporal[1], preferred_element_type=jnp.float32)
    total = total + jnp.dot(odd_frames, w_temporal[2], preferred_element_type=jnp.float32)
    return (total + b_temporal).astype(jnp.bfloat16)


def spatial_conv(padded, kernel, b_spatial, row_count, width, channels):
    frame_count = padded.shape[0]
    columns = jnp.concatenate(
        [padded[:, :, 0:width], padded[:, :, 1 : width + 1], padded[:, :, 2 : width + 2]], axis=-1
    )
    summed = jnp.zeros((frame_count, row_count, width, channels), jnp.float32) + b_spatial
    for row_tap in range(3):
        summed = summed + jnp.dot(
            columns[:, row_tap : row_tap + row_count],
            kernel[row_tap],
            preferred_element_type=jnp.float32,
        )
    return jax.nn.silu(summed).astype(jnp.bfloat16)


def per_device(video, w_spatial, b_spatial, w_temporal, b_temporal):
    frame_count, row_count, width, channels = video.shape
    kernel = w_spatial.reshape(3, 3 * channels, channels)
    padded = with_halo(video, (("rows", 1),), 1)
    padded = jnp.pad(padded, ((0, 0), (0, 0), (1, 1), (0, 0)))
    activated = spatial_conv(padded, kernel, b_spatial, row_count, width, channels)
    incoming = shifted(activated[frame_count - 1 :], "frames", 1)
    even_frames = activated[0::2]
    odd_frames = activated[1::2]
    prev_frames = jnp.concatenate([incoming, odd_frames[:-1]], axis=0)
    return temporal_mix(prev_frames, even_frames, odd_frames, w_temporal, b_temporal)


def solution(mesh):
    in_specs = (P(("batch", "frames"), "rows", None, None), P(), P(), P(), P())
    out_specs = P(("batch", "frames"), "rows", None, None)
    return jax.shard_map(
        per_device, mesh=mesh, in_specs=in_specs, out_specs=out_specs, check_vma=False
    )
```

profile of v0, /device:TPU:160, one launch (start us, length us, event | category | flops | bytes accessed | tf_op | source)
XLA Modules:
  0.0 116.9 jit_solution(16632257948775158530)
XLA Ops:
  0.0 0.0 copy-start
  0.0 1.2 fusion.14
  1.2 1.3 %collective-permute-start.1 = (bf16[2,1,128,320]{2,3,1,0:T(8,128)(2,1)S(1)}, bf16[2,1,128,320]{2,3,1,0:T(8,128)(2,1)S(1)}, u32[]{:S(2)}, u32[]{:S(2)}) collective-permute-start(bf16[2,1,128,320]{2,3,1,0:T(8,128)(2,1)S(1)} %get-tuple-element.7), channel_id=1, source_target_pairs={{4,0},{5,1},{6,2},{7,3},{12,8},{13,9},{14,10},{15,11},{20,16},{21,... | collective-permute-start | bytes 491528 | tf_op jit(solution)/shard_map/ppermute | solution.py:17
  2.5 3.0 %collective-permute-start = (bf16[2,1,128,320]{2,3,1,0:T(8,128)(2,1)S(1)}, bf16[2,1,128,320]{2,3,1,0:T(8,128)(2,1)S(1)}, u32[]{:S(2)}, u32[]{:S(2)}) collective-permute-start(bf16[2,1,128,320]{2,3,1,0:T(8,128)(2,1)S(1)} %get-tuple-element.8), channel_id=1, source_target_pairs={{0,4},{1,5},{2,6},{3,7},{8,12},{9,13},{10,14},{11,15},{16,20},{17,... | collective-permute-start | bytes 491528 | tf_op jit(solution)/shard_map/ppermute | solution.py:15
  5.5 1.8 %fusion.15 = (bf16[1,3,320,320]{3,2,1,0:T(8,128)(2,1)S(1)}, bf16[1,3,320,320]{3,2,1,0:T(8,128)(2,1)S(1)}, bf16[1,3,320,320]{3,2,1,0:T(8,128)(2,1)S(1)}) fusion(bf16[3,3,320,320]{3,2,1,0:T(8,128)(2,1)} %param.6), kind=kLoop, calls=%fused_computation.24 | loop fusion | bytes 3686400 | tf_op jit(solution)/shard_map/slice | solution.py:46
  7.3 0.0 collective-permute-done
  7.3 0.0 copy-done
  7.4 0.3 constant_dynamic-update-slice_fusion.1
  7.7 0.0 collective-permute-done.1
  7.8 1.7 %pad_slice_fusion.1 = (bf16[2,18,128,320]{2,3,1,0:T(8,128)(2,1)S(1)}, bf16[2,18,128,320]{2,3,1,0:T(8,128)(2,1)S(1)}) fusion(bf16[2,18,128,320]{2,3,1,0:T(8,128)(2,1)S(1)} %constant_dynamic-update-slice_fusion), kind=kLoop, calls=%fused_computation.2 | loop fusion | bytes 8847360 | tf_op jit(solution)/shard_map/slice | solution.py:40
  9.5 26.0 %fusion.12 = f32[2,16,128,320]{2,3,1,0:T(8,128)S(1)} fusion(bf16[960,320,1,1]{1,0,3,2:T(8,128)(2,1)S(1)} %bitcast.40, bf16[2,18,128,320]{2,3,1,0:T(8,128)(2,1)S(1)} %get-tuple-element.6, bf16[2,18,128,320]{2,3,1,0:T(8,128)(2,1)S(1)} %constant_dynamic-update-slice_fusion, bf16[2,18,128,320]{2,3,1,0:T(8,128)(2,1)S(1)} %get-tuple-element.5), kind=kOutput, calls=%fused_computation.21 | convolution fusion | flops 2543124480 | bytes 14704640 | tf_op jit(solution)/shard_map/dot_general | solution.py:44
  35.4 0.0 copy-start.3
  35.4 4.7 %fusion.13 = f32[2,16,128,320]{2,3,1,0:T(8,128)} fusion(bf16[960,320,1,1]{1,0,3,2:T(8,128)(2,1)S(1)} %bitcast.39, bf16[2,18,128,320]{2,3,1,0:T(8,128)(2,1)S(1)} %get-tuple-element.6, bf16[2,18,128,320]{2,3,1,0:T(8,128)(2,1)S(1)} %constant_dynamic-update-slice_fusion, bf16[2,18,128,320]{2,3,1,0:T(8,128)(2,1)S(1)} %get-tuple-element.5), kind=kOutput, calls=%fused_computation.22 | convolution fusion | flops 2543124480 | bytes 14704640 | tf_op jit(solution)/shard_map/dot_general | solution.py:44
  40.2 0.0 copy-done.3
  40.2 6.2 %multiply_convert_fusion = bf16[2,16,128,320]{2,3,1,0:T(8,128)(2,1)S(1)} fusion(f32[2,16,128,320]{2,3,1,0:T(8,128)S(1)} %fusion.12, f32[2,16,128,320]{2,3,1,0:T(8,128)} %fusion.13, f32[320]{0:T(512)S(1)} %copy-done.3, bf16[960,320,1,1]{1,0,3,2:T(8,128)(2,1)S(1)} %bitcast.38, bf16[2,18,128,320]{2,3,1,0:T(8,128)(2,1)S(1)} %get-tuple-element.6, ...), kind=kOutput, calls=%fused_computation.3 | convolution fusion | flops 2553610240 | bytes 22570240 | tf_op jit(solution)/shard_map/dot_general | solution.py:44
  46.4 0.1 slice.67
  46.5 3.4 %collective-permute-start.2 = (bf16[1,16,128,320]{2,3,1,0:T(8,128)(2,1)S(1)}, bf16[1,16,128,320]{2,3,1,0:T(8,128)(2,1)S(1)}, u32[]{:S(2)}, u32[]{:S(2)}) collective-permute-start(bf16[1,16,128,320]{2,3,1,0:T(8,128)(2,1)S(1)} %slice.67), channel_id=1, source_target_pairs={{0,8},{8,16},{16,24},{24,32},{32,40},{40,48},{48,56},{56,64},{64,7... | collective-permute-start | bytes 3932168 | tf_op jit(solution)/shard_map/ppermute | solution.py:27
  49.9 0.0 copy-done.1
  49.9 0.9 fusion.2
  50.8 0.0 copy-start.2
  50.8 0.9 fusion.1
  51.7 63.2 %collective-permute-done.2 = bf16[1,16,128,320]{2,3,1,0:T(8,128)(2,1)S(1)} collective-permute-done((bf16[1,16,128,320]{2,3,1,0:T(8,128)(2,1)S(1)}, bf16[1,16,128,320]{2,3,1,0:T(8,128)(2,1)S(1)}, u32[]{:S(2)}, u32[]{:S(2)}) %collective-permute-start.2) | collective-permute-done | bytes 1310752 | tf_op jit(solution)/shard_map/ppermute | solution.py:27
  114.9 0.0 copy-done.2
  114.9 2.0 %fusion = bf16[1,16,128,320]{2,3,1,0:T(8,128)(2,1)} fusion(f32[16,128,320]{1,2,0:T(8,128)S(1)} %fusion.2, f32[16,128,320]{1,2,0:T(8,128)S(1)} %fusion.1, bf16[1,16,128,320]{2,3,1,0:T(8,128)(2,1)S(1)} %collective-permute-done.2, f32[320]{0:T(512)S(1)} %copy-done.2, bf16[3,320,320]{2,1,0:T(8,128)(2,1)S(1)} %copy-done.1), kind=kOutput, calls=%fused_computation.5 | convolution fusion | flops 422051840 | bytes 8112128 | tf_op jit(solution)/shard_map/dot_general | solution.py:31
  (3 shorter events, 0.0 us)
Async XLA Ops:
  0.0 7.3 %copy-start = (bf16[2,16,128,320]{2,3,1,0:T(8,128)(2,1)S(1)}, bf16[2,16,128,320]{2,3,1,0:T(8,128)(2,1)}, u32[]{:S(2)}) copy-start(bf16[2,16,128,320]{2,3,1,0:T(8,128)(2,1)} %param.5) | copy-start | bytes 7864324
  1.2 6.5 %collective-permute-start.1 = (bf16[2,1,128,320]{2,3,1,0:T(8,128)(2,1)S(1)}, bf16[2,1,128,320]{2,3,1,0:T(8,128)(2,1)S(1)}, u32[]{:S(2)}, u32[]{:S(2)}) collective-permute-start(bf16[2,1,128,320]{2,3,1,0:T(8,128)(2,1)S(1)} %get-tuple-element.7), channel_id=1, source_target_pairs={{4,0},{5,1},{6,2},{7,3},{12,8},{13,9},{14,10},{15,11},{20,16},{21,... | collective-permute-start | bytes 491528 | tf_op jit(solution)/shard_map/ppermute | solution.py:17
  2.5 4.8 %collective-permute-start = (bf16[2,1,128,320]{2,3,1,0:T(8,128)(2,1)S(1)}, bf16[2,1,128,320]{2,3,1,0:T(8,128)(2,1)S(1)}, u32[]{:S(2)}, u32[]{:S(2)}) collective-permute-start(bf16[2,1,128,320]{2,3,1,0:T(8,128)(2,1)S(1)} %get-tuple-element.8), channel_id=1, source_target_pairs={{0,4},{1,5},{2,6},{3,7},{8,12},{9,13},{10,14},{11,15},{16,20},{17,... | collective-permute-start | bytes 491528 | tf_op jit(solution)/shard_map/ppermute | solution.py:15
  35.4 4.7 %copy-start.3 = (f32[320]{0:T(512)S(1)}, f32[320]{0:T(512)}, u32[]{:S(2)}) copy-start(f32[320]{0:T(512)} %param.7) | copy-start | bytes 3844
  40.2 9.8 %copy-start.1 = (bf16[3,320,320]{2,1,0:T(8,128)(2,1)S(1)}, bf16[3,320,320]{2,1,0:T(8,128)(2,1)}, u32[]{:S(2)}) copy-start(bf16[3,320,320]{2,1,0:T(8,128)(2,1)} %param.8) | copy-start | bytes 1843204
  46.5 68.4 %collective-permute-start.2 = (bf16[1,16,128,320]{2,3,1,0:T(8,128)(2,1)S(1)}, bf16[1,16,128,320]{2,3,1,0:T(8,128)(2,1)S(1)}, u32[]{:S(2)}, u32[]{:S(2)}) collective-permute-start(bf16[1,16,128,320]{2,3,1,0:T(8,128)(2,1)S(1)} %slice.67), channel_id=1, source_target_pairs={{0,8},{8,16},{16,24},{24,32},{32,40},{40,48},{48,56},{56,64},{64,7... | collective-permute-start | bytes 3932168 | tf_op jit(solution)/shard_map/ppermute | solution.py:27
  50.8 64.1 %copy-start.2 = (f32[320]{0:T(512)S(1)}, f32[320]{0:T(512)}, u32[]{:S(2)}) copy-start(f32[320]{0:T(512)} %param.9) | copy-start | bytes 3844
where the time goes:
time: 117 us
  waiting for transfers between devices  63.2 us (54%)
  matrix products  40.7 us (35%)
  starting transfers between devices  7.73 us (7%)
  local copies, waits for them, and re-layouts  5.15 us (4%)
    ppermute x1, waiting for transfers between devices, shifted(): return lax.ppermute(block, axis, route)  63.2 us
    dot_general x3, matrix products, spatial_conv(): jnp.dot(columns[:, row_tap:row_tap + row_count], kernel[row_tap], preferr...  36.9 us
    ppermute x1, starting transfers between devices, shifted(): return lax.ppermute(block, axis, route)  3.39 us
    ppermute x1, starting transfers between devices, with_halo(): lax.ppermute(tail, axis, [(i, (i + 1) % count) for i in range(ends)])  3.05 us
  transfers between devices with their start and end apart: 3, of which 1 were waited for; matrix products, arithmetic and copies ran while one was open for 3% of the time, Pallas kernels for 0%

commit v1 on v0

v1 whole, which is shorter than its diff:
```python
import functools

import jax
import jax.numpy as jnp
from jax import lax
from jax.experimental import pallas as pl
from jax.experimental.pallas import tpu as pltpu
from jax.sharding import PartitionSpec as P

MESH = pl.DeviceIdType.MESH
F32 = jnp.float32
BF16 = jnp.bfloat16

LONG = (0, 2, 4, 6)
LONG_AT = (6, 9, 12, 15)
CROSS = {
    "direct": (13, 15),
    "a1": (5, 11),
    "b0": (0, 4, 8, 12),
    "b1": (1, 7),
    "c0": (2, 6, 10, 14),
    "c1": (3, 9),
}
CROSS_LAG = 4
LAST = ((1, 3), (5, 7), (8, 9), (0, 2), (10, 11), (12, 13), (4, 6), (14, 15))


def shifted_add(z, channels, width, lane):
    left, mid, right = z[:channels], z[channels : 2 * channels], z[2 * channels :]

    def roll(block, amount):
        return jnp.concatenate(
            [pltpu.roll(block[:, s * width : (s + 1) * width], amount, 1) for s in range(2)], axis=1
        )

    mid = mid + jnp.where(lane == 0, 0.0, roll(left, 1))
    return mid + jnp.where(lane == width - 1, 0.0, roll(right, width - 1))


def kernel(
    v_hbm, ws_hbm, bs_ref, wt_hbm, bt_ref, o_hbm,
    vbuf, wraw, traw, wmat, tmat, act, even, prev, acc, obuf, bias, longbuf, crossbuf,
    load_sem, halo_send, halo_recv, send_sem, prev_recv, long_recv, long_send, cross_recv, cross_send, out_sem,
):
    rows, channels, width = act.shape
    f, r, zl = lax.axis_index("frames"), lax.axis_index("rows"), lax.axis_index("batch")
    zh, y, x = f // 16, (f // 4) % 4, f % 4
    z = zh * 4 + zl
    turn = (z + 7 + 2 * (z % 2)) % 8
    source_z = turn

    def chip(cx, cy, cz):
        return (cz // 4 * 16 + cy * 4 + cx, r, cz % 4)

    def remote(src, dst, ssem, rsem, to):
        return pltpu.make_async_remote_copy(
            src_ref=src, dst_ref=dst, send_sem=ssem, recv_sem=rsem, device_id=to, device_id_type=MESH
        )

    odd_in = pltpu.make_async_copy(v_hbm.at[1], vbuf.at[1, pl.ds(1, rows)], load_sem.at[0])
    even_in = pltpu.make_async_copy(v_hbm.at[0], vbuf.at[0, pl.ds(1, rows)], load_sem.at[1])
    ws_in = pltpu.make_async_copy(ws_hbm, wraw, load_sem.at[2])
    wt_in = pltpu.make_async_copy(wt_hbm, traw, load_sem.at[3])
    ws_in.start()
    odd_in.start()
    even_in.start()
    wt_in.start()

    sends = jnp.logical_and(f != 15, f != 31)
    takes = jnp.logical_and(f != 0, f != 16)
    is_relay = x % 2 == 1
    far_origin = jnp.logical_not(jnp.logical_and(x == 1, y == 3))
    is_source = f == 15
    is_target = f == 16
    low = zh == 0
    turned = jnp.logical_or(jnp.logical_or(z == 7, z == 4), jnp.logical_or(z == 1, z == 2))
    corner_a = jnp.logical_and(x == 3, y == 3)
    corner_b = jnp.logical_and(x == 0, y == 3)
    corner_c = jnp.logical_and(x == 0, y == 0)
    roles = {
        "a1": jnp.logical_and(corner_a, turned),
        "b0": jnp.logical_and(corner_b, low),
        "b1": jnp.logical_and(corner_b, turned),
        "c0": jnp.logical_and(corner_c, low),
        "c1": jnp.logical_and(corner_c, turned),
    }
    spots = {"a1": (3, 3, 1), "b0": (0, 3, 0), "b1": (0, 3, 1), "c0": (0, 0, 0), "c1": (0, 0, 1)}
    next_frames = (f + 1, r, zl)
    sibling = (f, 1 - r, zl)
    relay = chip((x + 3 - x % 2) % 4, y, z)
    near_target = chip((x + 2) % 4, y, z)
    far_target = chip((x + 3) % 4, y + (3 - x) // 2, z)

    barrier = pltpu.get_barrier_semaphore()

    def tell(who):
        pl.semaphore_signal(barrier, inc=1, device_id=who, device_id_type=MESH)

    tell(sibling)

    @pl.when(takes)
    def _():
        before = f - 1
        bx, by = before % 4, (before // 4) % 4
        tell((before, r, zl))
        tell(chip((bx + 3 - bx % 2) % 4, by, z))

    @pl.when(is_relay)
    def _():
        tell(chip((x + 1) % 4, y, z))

    @pl.when(jnp.logical_and(is_relay, far_origin))
    def _():
        tell(chip((x + 2) % 4, y, z))

    for name, role in roles.items():

        @pl.when(role)
        def _(turned_here=spots[name][2]):
            tell(chip(3, 3, source_z if turned_here else z))

    @pl.when(is_target)
    def _():
        s = z - 4
        s_turn = (s + 7 + 2 * (s % 2)) % 8
        tell(chip(3, 3, s))
        for sx, sy, t in spots.values():
            tell(chip(sx, sy, s_turn if t else s))

    def count(condition, number=1):
        return condition.astype(jnp.int32) * number

    expected = 1 + count(sends, 2) + count(is_relay) + count(jnp.logical_and(is_relay, far_origin))
    expected = expected + count(is_source, 6)
    for role in roles.values():
        expected = expected + count(role)
    pl.semaphore_wait(barrier, expected)

    halos = [
        remote(
            v_hbm.at[i, (rows - 1) * (1 - r)],
            vbuf.at[i, (rows + 1) * r],
            halo_send.at[i],
            halo_recv.at[i],
            sibling,
        )
        for i in range(2)
    ]
    halos[1].start()
    halos[0].start()
    for i in range(2):
        vbuf[i, (rows + 1) * r] = jnp.zeros((channels, width), BF16)

    eye = lax.broadcasted_iota(jnp.int32, (channels, channels), 0) == lax.broadcasted_iota(
        jnp.int32, (channels, channels), 1
    )
    for i, ref in enumerate((bs_ref, bt_ref)):
        column = jnp.sum(jnp.where(eye, ref[...], 0.0), axis=1, keepdims=True)
        bias[i] = jnp.broadcast_to(column, (channels, 2 * width))

    ws_in.wait()
    for i in range(3):
        for j in range(3):
            wmat[j * channels : (j + 1) * channels, i * channels : (i + 1) * channels] = wraw[i, j].T
    odd_in.wait()
    halos[1].wait()

    lane = lax.broadcasted_iota(jnp.int32, (channels, 2 * width), 1) % width

    def spatial(i, h):
        lines = [vbuf[i, h + k] for k in range(4)]
        rhs = jnp.concatenate(
            [jnp.concatenate([lines[k], lines[k + 1]], axis=1) for k in range(3)], axis=0
        )
        total = jnp.dot(wmat[...], rhs, preferred_element_type=F32)
        total = shifted_add(total, channels, width, lane) + bias[0]
        return (total / (1.0 + jnp.exp(-total))).astype(BF16)

    def direct(h):
        return remote(act.at[h], prev.at[h], send_sem.at[h], prev_recv.at[h], next_frames)

    def long_first(k):
        return remote(
            act.at[LONG[k]], longbuf.at[x % 2, k], send_sem.at[LONG[k]], long_recv.at[x % 2, k], relay
        )

    def long_second(slot, k):
        to = far_target if slot else near_target
        return remote(
            longbuf.at[slot, k], prev.at[LONG[k]], long_send.at[slot, k], prev_recv.at[LONG[k]], to
        )

    def cross_first(name, h):
        if name == "direct":
            return remote(act.at[h], prev.at[h], send_sem.at[h], prev_recv.at[h], chip(0, 0, z + 4))
        sx, sy, t = spots[name]
        return remote(
            act.at[h], crossbuf.at[h], send_sem.at[h], cross_recv.at[h], chip(sx, sy, turn if t else z)
        )

    def cross_second(name, h):
        s = source_z if spots[name][2] else z
        return remote(crossbuf.at[h], prev.at[h], cross_send.at[h], prev_recv.at[h], chip(0, 0, s + 4))

    def first_sends(t):
        for h in (2 * t, 2 * t + 1):

            @pl.when(sends)
            def _(h=h):
                (long_first(LONG.index(h)) if h in LONG else direct(h)).start()

            @pl.when(is_source)
            def _(h=h):
                for name, taken in CROSS.items():
                    if h in taken:
                        cross_first(name, h).start()

    def second_sends(t):
        for k, at in enumerate(LONG_AT):
            if at == t:

                @pl.when(is_relay)
                def _(k=k):
                    pltpu.make_async_copy(longbuf.at[0, k], longbuf.at[0, k], long_recv.at[0, k]).wait()
                    long_second(0, k).start()

                @pl.when(jnp.logical_and(is_relay, far_origin))
                def _(k=k):
                    pltpu.make_async_copy(longbuf.at[1, k], longbuf.at[1, k], long_recv.at[1, k]).wait()
                    long_second(1, k).start()

        for name, role in roles.items():
            for h in CROSS[name]:
                if h // 2 + CROSS_LAG == t:

                    @pl.when(role)
                    def _(name=name, h=h):
                        pltpu.make_async_copy(crossbuf.at[h], crossbuf.at[h], cross_recv.at[h]).wait()
                        cross_second(name, h).start()

    @pl.loop(0, rows)
    def _(t):
        i = 1 - t // (rows // 2)
        h = t % (rows // 2) * 2

        @pl.when(t == rows // 2)
        def _():
            even_in.wait()
            halos[0].wait()

        out = spatial(i, h)

        @pl.when(i == 1)
        def _():
            act[h] = out[:, :width]
            act[h + 1] = out[:, width:]

        @pl.when(i == 0)
        def _():
            even[h] = out[:, :width]
            even[h + 1] = out[:, width:]

        for at in range(rows):

            @pl.when(t == at)
            def _(at=at):
                if at < rows // 2:
                    first_sends(at)
                second_sends(at)

    wt_in.wait()
    tmat[:, 0:channels] = traw[1].T
    tmat[:, channels : 2 * channels] = traw[2].T
    tmat[:, 2 * channels :] = traw[0].T

    @pl.loop(0, rows // 2)
    def _(t):
        h = t * 2
        rhs = jnp.concatenate(
            [
                jnp.concatenate([even[h], even[h + 1]], axis=1),
                jnp.concatenate([act[h], act[h + 1]], axis=1),
            ],
            axis=0,
        )
        part = jnp.dot(tmat[:, : 2 * channels], rhs, preferred_element_type=F32) + bias[1]
        acc[h] = part[:, :width]
        acc[h + 1] = part[:, width:]

    gets = f != 0
    for pair in LAST:
        for h in pair:

            @pl.when(gets)
            def _(h=h):
                pltpu.make_async_copy(prev.at[h], prev.at[h], prev_recv.at[h]).wait()

        a, b = pair

        @pl.when(gets)
        def _(a=a, b=b):
            rhs = jnp.concatenate([prev[a], prev[b]], axis=1)
            part = jnp.dot(tmat[:, 2 * channels :], rhs, preferred_element_type=F32)
            obuf[a] = (acc[a] + part[:, :width]).astype(BF16)
            obuf[b] = (acc[b] + part[:, width:]).astype(BF16)

        @pl.when(jnp.logical_not(gets))
        def _(a=a, b=b):
            obuf[a] = acc[a].astype(BF16)
            obuf[b] = acc[b].astype(BF16)

        for h in pair:
            pltpu.make_async_copy(obuf.at[h], o_hbm.at[h], out_sem.at[h]).start()

    @pl.when(sends)
    def _():
        for h in range(rows):
            direct(h).wait_send()

    @pl.when(is_source)
    def _():
        for h in range(rows):
            direct(h).wait_send()

    for k in range(len(LONG)):

        @pl.when(is_relay)
        def _(k=k):
            long_second(0, k).wait_send()

        @pl.when(jnp.logical_and(is_relay, far_origin))
        def _(k=k):
            long_second(1, k).wait_send()

    for name, role in roles.items():
        for h in CROSS[name]:

            @pl.when(role)
            def _(name=name, h=h):
                cross_second(name, h).wait_send()

    for h in range(rows):
        pltpu.make_async_copy(obuf.at[h], o_hbm.at[h], out_sem.at[h]).wait()


def per_device(video, w_spatial, b_spatial, w_temporal, b_temporal):
    frames, rows, width, channels = video.shape
    dma = pltpu.SemaphoreType.DMA
    out = pl.pallas_call(
        kernel,
        out_shape=jax.ShapeDtypeStruct((rows, channels, width), BF16),
        in_specs=[
            pl.BlockSpec(memory_space=pl.ANY),
            pl.BlockSpec(memory_space=pl.ANY),
            pl.BlockSpec(memory_space=pltpu.VMEM),
            pl.BlockSpec(memory_space=pl.ANY),
            pl.BlockSpec(memory_space=pltpu.VMEM),
        ],
        out_specs=pl.BlockSpec(memory_space=pl.ANY),
        scratch_shapes=[
            pltpu.VMEM((frames, rows + 2, channels, width), BF16),
            pltpu.VMEM(w_spatial.shape, BF16),
            pltpu.VMEM(w_temporal.shape, BF16),
            pltpu.VMEM((3 * channels, 3 * channels), BF16),
            pltpu.VMEM((channels, 3 * channels), BF16),
            pltpu.VMEM((rows, channels, width), BF16),
            pltpu.VMEM((rows, channels, width), BF16),
            pltpu.VMEM((rows, channels, width), BF16),
            pltpu.VMEM((rows, channels, width), F32),
            pltpu.VMEM((rows, channels, width), BF16),
            pltpu.VMEM((2, channels, 2 * width), F32),
            pltpu.VMEM((2, len(LONG), channels, width), BF16),
            pltpu.VMEM((rows, channels, width), BF16),
            dma((4,)),
            dma((2,)),
            dma((2,)),
            dma((rows,)),
            dma((rows,)),
            dma((2, len(LONG))),
            dma((2, len(LONG))),
            dma((rows,)),
            dma((rows,)),
            dma((rows,)),
        ],
        compiler_params=pltpu.CompilerParams(
            collective_id=0, has_side_effects=True, vmem_limit_bytes=60 * 1024 * 1024
        ),
        name="level",
    )(
        jnp.swapaxes(video, 2, 3),
        w_spatial,
        b_spatial,
        w_temporal,
        b_temporal,
    )
    return jnp.swapaxes(out, 1, 2)[None]


def solution(mesh):
    in_specs = (P(("batch", "frames"), "rows", None, None), P(), P(), P(), P())
    out_specs = P(("batch", "frames"), "rows", None, None)
    return jax.shard_map(
        per_device, mesh=mesh, in_specs=in_specs, out_specs=out_specs, check_vma=False
    )
```

time: 117 us -> 50.9 us (0.44)
  the two profiles are of different devices: /device:TPU:160 before, /device:TPU:128 now
where the time goes in v1:
time: 50.9 us; the launch traced here: 50.8 us
  Pallas kernels  48.3 us (95%)
  local copies, waits for them, and re-layouts  2.47 us (5%)
    pallas_call x1, Pallas kernels, per_device(): pl.pallas_call(kernel, out_shape=jax.ShapeDtypeStruct((rows, channels, wi...  48.3 us
    unnamed x1, local copies, waits for them, and re-layouts  2.47 us

profile of v1, /device:TPU:128, one launch (start us, length us, event | category | flops | bytes accessed | tf_op | source)
XLA Modules:
  0.0 50.8 jit_solution(16217298156983882800)
XLA Ops:
  0.0 48.3 %level.1 = bf16[16,320,128]{2,1,0:T(8,128)(2,1)} custom-call(bf16[2,16,320,128]{3,2,1,0:T(8,128)(2,1)} %bitcast.5, bf16[3,3,320,320]{3,2,1,0:T(8,128)(2,1)} %ws_hbm.1, f32[320]{0:T(512)} %bs_ref.1, bf16[3,320,320]{2,1,0:T(8,128)(2,1)} %wt_hbm.1, f32[320]{0:T(512)} %bt_ref.1), custom_call_target="tpu_custom_call" | custom-call | tf_op jit(solution)/shard_map/level/pallas_call | solution.py:349
  48.3 2.5 %copy.7 = bf16[1,16,128,320]{2,3,1,0:T(8,128)(2,1)} copy(bf16[1,16,128,320]{2,3,1,0:T(8,128)(2,1)} %bitcast.4) | data formatting | bytes 2621440

commit v2 on v1

v2 whole, which is shorter than its diff:
```python
import functools

import jax
import jax.numpy as jnp
from jax import lax
from jax.experimental import pallas as pl
from jax.experimental.pallas import tpu as pltpu
from jax.sharding import PartitionSpec as P

SPAN = 4
MAIN = 256
ONES = 16
GROUP = 16
MESH = pl.DeviceIdType.MESH
F32 = jnp.float32
BF16 = jnp.bfloat16

STEPS = ((1, 4), (1, 8), (1, 0), (1, 12), (0, 4), (0, 8), (0, 0), (0, 12))
LONG = (4, 6, 8, 10)
CROSS = {
    "direct": (8, 10, 3, 12, 15),
    "c1": (4,),
    "b0": (6, 13),
    "c0": (9, 0, 2, 14),
    "e0": (5, 7, 11, 1),
}
BETWEEN = {
    4: (("long", (0, 0)), ("cross", (4, 5))),
    5: (("long", (0, 1)), ("cross", (6,))),
    6: (("long", (0, 2)),),
    7: (("long", (0, 3)), ("cross", (7, 9))),
}
AFTER = (
    ("long", (1, 0)), ("pair", (5, 7)), ("pair", (9, 11)), ("cross", (11,)), ("long", (1, 1)), ("pair", (0, 1)),
    ("cross", (0,)), ("long", (1, 2)), ("cross", (1,)), ("long", (1, 3)), ("pair", (2, 3)), ("cross", (2, 13)),
    ("pair", (12, 13)), ("pair", (4, 6)), ("cross", (14,)), ("pair", (8, 10)), ("pair", (14, 15)),
)


def shifted_add(z, channels, width, lane):
    left, mid, right = (z[:, j].reshape(channels, SPAN * width) for j in range(3))

    def roll(block, amount):
        return jnp.concatenate(
            [pltpu.roll(block[:, s * width : (s + 1) * width], amount, 1) for s in range(SPAN)], axis=1
        )

    mid = mid + jnp.where(lane == 0, 0.0, roll(left, 1))
    return mid + jnp.where(lane == width - 1, 0.0, roll(right, width - 1))


def kernel(
    v_hbm, ws_hbm, bs_ref, wt_hbm, bt_ref, o_hbm,
    vbuf, wraw, traw, wmat, tmat, act, even, prev, obuf, za, zb, longbuf, crossbuf,
    load_sem, halo_send, halo_recv, send_sem, prev_recv, long_recv, long_send, cross_recv, cross_send, out_sem,
):
    rows, channels, width = act.shape
    groups = channels // GROUP
    f, r, zl = lax.axis_index("frames"), lax.axis_index("rows"), lax.axis_index("batch")
    zh, y, x = f // 16, (f // 4) % 4, f % 4
    z = zh * 4 + zl
    turn = (z + 7 + 2 * (z % 2)) % 8
    source_z = turn

    def chip(cx, cy, cz):
        return (cz // 4 * 16 + cy * 4 + cx, r, cz % 4)

    def remote(src, dst, ssem, rsem, to):
        return pltpu.make_async_remote_copy(
            src_ref=src, dst_ref=dst, send_sem=ssem, recv_sem=rsem, device_id=to, device_id_type=MESH
        )

    ws_in = [
        pltpu.make_async_copy(ws_hbm.at[:, j], wraw.at[:, j], load_sem.at[j]) for j in range(3)
    ]
    odd_in = pltpu.make_async_copy(v_hbm.at[1], vbuf.at[1, pl.ds(1, rows)], load_sem.at[3])
    even_in = pltpu.make_async_copy(v_hbm.at[0], vbuf.at[0, pl.ds(1, rows)], load_sem.at[4])
    wt_in = pltpu.make_async_copy(wt_hbm, traw, load_sem.at[5])
    for copy in (ws_in[0], ws_in[1], ws_in[2], odd_in, even_in, wt_in):
        copy.start()

    sends = jnp.logical_and(f != 15, f != 31)
    takes = jnp.logical_and(f != 0, f != 16)
    first_relay = jnp.logical_not(jnp.logical_and(x == 2, y == 0))
    second_relay = jnp.logical_not(jnp.logical_and(x == 1, y == 0))
    is_source = f == 15
    is_target = f == 16
    low = zh == 0
    turned = jnp.logical_or(jnp.logical_or(z == 7, z == 4), jnp.logical_or(z == 1, z == 2))
    corner_b = jnp.logical_and(x == 0, y == 3)
    corner_c = jnp.logical_and(x == 0, y == 0)
    corner_e = jnp.logical_and(x == 0, y == 1)
    roles = {
        "c1": jnp.logical_and(corner_c, turned),
        "b0": jnp.logical_and(corner_b, low),
        "c0": jnp.logical_and(corner_c, low),
        "e0": jnp.logical_and(corner_e, low),
    }
    spots = {"c1": (0, 0, 1), "b0": (0, 3, 0), "c0": (0, 0, 0), "e0": (0, 1, 0)}
    next_frames = (f + 1, r, zl)
    sibling = (f, 1 - r, zl)
    left = chip((x + 3) % 4, y, z)
    right = chip((x + 1) % 4, y, z)
    long_start = chip((x + 3) % 4, y + x // 3, z)
    long_origin = chip((x + 1) % 4, y - (x + 1) % 4 // 3, z)

    barrier = pltpu.get_barrier_semaphore()

    def tell(who):
        pl.semaphore_signal(barrier, inc=1, device_id=who, device_id_type=MESH)

    tell(sibling)

    @pl.when(takes)
    def _():
        tell((f - 1, r, zl))
        tell(right)

    @pl.when(first_relay)
    def _():
        tell(long_origin)

    @pl.when(second_relay)
    def _():
        tell(right)

    for name, role in roles.items():

        @pl.when(role)
        def _(turned_here=spots[name][2]):
            tell(chip(3, 3, source_z if turned_here else z))

    @pl.when(is_target)
    def _():
        s = z - 4
        s_turn = (s + 7 + 2 * (s % 2)) % 8
        tell(chip(3, 3, s))
        for sx, sy, t in spots.values():
            tell(chip(sx, sy, s_turn if t else s))

    def count(condition, number=1):
        return condition.astype(jnp.int32) * number

    expected = 1 + count(sends, 2) + count(first_relay) + count(second_relay)
    expected = expected + count(is_source, 1 + len(roles))
    for role in roles.values():
        expected = expected + count(role)
    def turned_about(blocks, bias_ref):
        if bias_ref is None:
            last = jnp.zeros((ONES, channels), BF16)
        else:
            parts, left = [], jnp.reshape(bias_ref[...], (1, channels))
            for _ in range(3):
                parts.append(left.astype(BF16).astype(F32))
                left = left - parts[-1]
            row = lax.broadcasted_iota(jnp.int32, (ONES, channels), 0)
            last = jnp.zeros((ONES, channels), F32)
            for k, part in enumerate(parts):
                last = jnp.where(row == k, jnp.broadcast_to(part, (ONES, channels)), last)
            last = last.astype(BF16)
        for block in blocks:
            yield block[:MAIN].T
        yield jnp.concatenate([block[MAIN:] for block in blocks] + [last], axis=0).T

    for j in range(3):
        ws_in[j].wait()
        blocks = [wraw.at[i, j] for i in range(3)]
        at = 0
        for piece in turned_about(blocks, bs_ref if j == 1 else None):
            size = piece.shape[1]
            wmat[:, j, :, at : at + size] = piece.reshape(groups, GROUP, size)
            at += size

    pl.semaphore_wait(barrier, expected)
    halos = [
        remote(
            v_hbm.at[i, (rows - 1) * (1 - r)],
            vbuf.at[i, (rows + 1) * r],
            halo_send.at[i],
            halo_recv.at[i],
            sibling,
        )
        for i in range(2)
    ]
    halos[1].start()
    halos[0].start()
    for i in range(2):
        vbuf[i, (rows + 1) * r] = jnp.zeros((channels, width), BF16)
    odd_in.wait()

    lane = lax.broadcasted_iota(jnp.int32, (channels, SPAN * width), 1) % width
    depth = 3 * channels + ONES

    def stacked(rows_of):
        columns = len(rows_of) * width
        ones = (lax.broadcasted_iota(jnp.int32, (ONES, columns), 0) < 3).astype(F32).astype(BF16)
        return jnp.concatenate(
            [
                jnp.concatenate([lines[k][part] for lines in rows_of], axis=1)
                for part in (slice(0, MAIN), slice(MAIN, None))
                for k in range(3)
            ]
            + [ones],
            axis=0,
        )

    def taps(i, h):
        lines = [vbuf[i, h + k] for k in range(SPAN + 2)]
        return jnp.dot(
            wmat[...].reshape(3 * channels, depth),
            stacked([lines[k : k + 3] for k in range(SPAN)]),
            preferred_element_type=F32,
        )

    def finish(taken, out, h):
        total = shifted_add(taken.reshape(groups, 3, GROUP, SPAN * width), channels, width, lane)
        total = (total / (1.0 + jnp.exp(-total))).astype(BF16)
        for k in range(SPAN):
            out[h + k] = total[:, k * width : (k + 1) * width]

    def direct(h):
        return remote(act.at[h], prev.at[h], send_sem.at[h], prev_recv.at[h], next_frames)

    def long_first(k):
        h = LONG[k]
        return remote(act.at[h], longbuf.at[0, k], send_sem.at[h], long_recv.at[0, k], long_start)

    def long_next(stage, k):
        there, arrived = (
            (longbuf.at[1, k], long_recv.at[1, k]) if stage == 0 else (prev.at[LONG[k]], prev_recv.at[LONG[k]])
        )
        return remote(longbuf.at[stage, k], there, long_send.at[stage, k], arrived, left)

    def cross_first(name, h):
        if name == "direct":
            return remote(act.at[h], prev.at[h], send_sem.at[h], prev_recv.at[h], chip(0, 0, z + 4))
        sx, sy, t = spots[name]
        return remote(
            act.at[h], crossbuf.at[h], send_sem.at[h], cross_recv.at[h], chip(sx, sy, turn if t else z)
        )

    def cross_second(name, h):
        s = source_z if spots[name][2] else z
        return remote(crossbuf.at[h], prev.at[h], cross_send.at[h], prev_recv.at[h], chip(0, 0, s + 4))

    def first_sends(first):
        for h in range(first, first + SPAN):

            @pl.when(sends)
            def _(h=h):
                (long_first(LONG.index(h)) if h in LONG else direct(h)).start()

            @pl.when(is_source)
            def _(h=h):
                for name, taken in CROSS.items():
                    if h in taken:
                        cross_first(name, h).start()

    def long_pass(stage, k):
        @pl.when((first_relay, second_relay)[stage])
        def _():
            pltpu.make_async_copy(longbuf.at[stage, k], longbuf.at[stage, k], long_recv.at[stage, k]).wait()
            long_next(stage, k).start()

    def cross_pass(taken):
        for name, role in roles.items():
            mine = [h for h in taken if h in CROSS[name]]
            if mine:

                @pl.when(role)
                def _(name=name, mine=mine):
                    for h in mine:
                        pltpu.make_async_copy(crossbuf.at[h], crossbuf.at[h], cross_recv.at[h]).wait()
                        cross_second(name, h).start()

    def temporal(pair):
        @pl.when(gets)
        def _():
            for h in pair:
                pltpu.make_async_copy(prev.at[h], prev.at[h], prev_recv.at[h]).wait()

        rhs = stacked([[ref[h] for ref in (prev, even, act)] for h in pair])
        total = jnp.dot(tmat[...], rhs, preferred_element_type=F32).astype(BF16)
        for k, h in enumerate(pair):
            obuf[h] = total[:, k * width : (k + 1) * width]
            pltpu.make_async_copy(obuf.at[h], o_hbm.at[h], out_sem.at[h]).start()

    finish(taps(*STEPS[0]), act, STEPS[0][1])
    first_sends(STEPS[0][1])
    za[...] = taps(*STEPS[1])
    here, there = za, zb
    for n in range(2, len(STEPS) + 1):
        if n < len(STEPS):
            if STEPS[n][1] in (0, rows - SPAN) and STEPS[n - 1][1] not in (0, rows - SPAN):
                halos[STEPS[n][0]].wait_recv()
            if STEPS[n][0] != STEPS[n - 1][0]:
                even_in.wait()
            there[...] = taps(*STEPS[n])
        else:
            wt_in.wait()
            at = 0
            for piece in turned_about([traw.at[k] for k in range(3)], bt_ref):
                tmat[:, at : at + piece.shape[1]] = piece
                at += piece.shape[1]
        i, h = STEPS[n - 1]
        finish(here[...], act if i else even, h)
        if i:
            first_sends(h)
        here, there = there, here
        for kind, what in BETWEEN.get(n, ()):
            if kind == "long":
                long_pass(*what)
            else:
                cross_pass(what)

    @pl.when(f == 0)
    def _():
        prev[...] = jnp.zeros_like(prev)

    gets = f != 0
    for kind, what in AFTER:
        if kind == "long":
            long_pass(*what)
        elif kind == "cross":
            cross_pass(what)
        else:

            @pl.when(jnp.logical_not(is_target))
            def _(what=what):
                temporal(what)

    @pl.when(is_target)
    def _():
        @pl.loop(0, rows // 2)
        def _(t):
            inner = jnp.logical_and(t >= 4, t < 6).astype(jnp.int32)
            h = 2 * t + 4 - 12 * inner - 4 * (t >= 6).astype(jnp.int32)
            temporal((h, h + 1))

    for i in range(2):
        halos[i].wait_send()

    @pl.when(sends)
    def _():
        for h in range(rows):
            direct(h).wait_send()

    @pl.when(is_source)
    def _():
        for h in range(rows):
            direct(h).wait_send()

    for stage, role in enumerate((first_relay, second_relay)):

        @pl.when(role)
        def _(stage=stage):
            for k in range(len(LONG)):
                long_next(stage, k).wait_send()

    for name, role in roles.items():
        for h in CROSS[name]:

            @pl.when(role)
            def _(name=name, h=h):
                cross_second(name, h).wait_send()

    for h in range(rows):
        pltpu.make_async_copy(obuf.at[h], o_hbm.at[h], out_sem.at[h]).wait()


def per_device(video, w_spatial, b_spatial, w_temporal, b_temporal):
    frames, rows, width, channels = video.shape
    dma = pltpu.SemaphoreType.DMA
    out = pl.pallas_call(
        kernel,
        out_shape=jax.ShapeDtypeStruct((rows, channels, width), BF16),
        in_specs=[
            pl.BlockSpec(memory_space=pl.ANY),
            pl.BlockSpec(memory_space=pl.ANY),
            pl.BlockSpec(memory_space=pltpu.VMEM),
            pl.BlockSpec(memory_space=pl.ANY),
            pl.BlockSpec(memory_space=pltpu.VMEM),
        ],
        out_specs=pl.BlockSpec(memory_space=pl.ANY),
        scratch_shapes=[
            pltpu.VMEM((frames, rows + 2, channels, width), BF16),
            pltpu.VMEM(w_spatial.shape, BF16),
            pltpu.VMEM(w_temporal.shape, BF16),
            pltpu.VMEM((channels // GROUP, 3, GROUP, 3 * channels + ONES), BF16),
            pltpu.VMEM((channels, 3 * channels + ONES), BF16),
            pltpu.VMEM((rows, channels, width), BF16),
            pltpu.VMEM((rows, channels, width), BF16),
            pltpu.VMEM((rows, channels, width), BF16),
            pltpu.VMEM((rows, channels, width), BF16),
            pltpu.VMEM((3 * channels, SPAN * width), F32),
            pltpu.VMEM((3 * channels, SPAN * width), F32),
            pltpu.VMEM((2, len(LONG), channels, width), BF16),
            pltpu.VMEM((rows, channels, width), BF16),
            dma((6,)),
            dma((2,)),
            dma((2,)),
            dma((rows,)),
            dma((rows,)),
            dma((2, len(LONG))),
            dma((2, len(LONG))),
            dma((rows,)),
            dma((rows,)),
            dma((rows,)),
        ],
        compiler_params=pltpu.CompilerParams(
            collective_id=0, has_side_effects=True, vmem_limit_bytes=60 * 1024 * 1024
        ),
        name="level",
    )(
        jnp.swapaxes(video, 2, 3),
        w_spatial,
        b_spatial,
        w_temporal,
        b_temporal,
    )
    return jnp.swapaxes(out, 1, 2)[None]


def solution(mesh):
    in_specs = (P(("batch", "frames"), "rows", None, None), P(), P(), P(), P())
    out_specs = P(("batch", "frames"), "rows", None, None)
    return jax.shard_map(
        per_device, mesh=mesh, in_specs=in_specs, out_specs=out_specs, check_vma=False
    )
```

time: 50.9 us -> 40.7 us (0.80)
  the two profiles are of different devices: /device:TPU:128 before, /device:TPU:160 now
where the time goes in v2:
time: 40.7 us; the launch traced here: 40.5 us
  Pallas kernels  38 us (93%)
  local copies, waits for them, and re-layouts  2.47 us (6%)
    pallas_call x1, Pallas kernels, per_device(): pl.pallas_call(kernel, out_shape=jax.ShapeDtypeStruct((rows, channels, wi...  38 us
    unnamed x1, local copies, waits for them, and re-layouts  2.47 us

profile of v2, /device:TPU:160, one launch (start us, length us, event | category | flops | bytes accessed | tf_op | source)
XLA Modules:
  0.0 40.5 jit_solution(16591108662605043741)
XLA Ops:
  0.0 38.0 %level.1 = bf16[16,320,128]{2,1,0:T(8,128)(2,1)} custom-call(bf16[2,16,320,128]{3,2,1,0:T(8,128)(2,1)} %bitcast.5, bf16[3,3,320,320]{3,2,1,0:T(8,128)(2,1)} %ws_hbm.1, f32[320]{0:T(512)} %bs_ref.1, bf16[3,320,320]{2,1,0:T(8,128)(2,1)} %wt_hbm.1, f32[320]{0:T(512)} %bt_ref.1), custom_call_target="tpu_custom_call" | custom-call | tf_op jit(solution)/shard_map/level/pallas_call | solution.py:374
  38.1 2.5 %copy.7 = bf16[1,16,128,320]{2,3,1,0:T(8,128)(2,1)} copy(bf16[1,16,128,320]{2,3,1,0:T(8,128)(2,1)} %bitcast.4) | data formatting | bytes 2621440

commit v3 on v2

--- a/solution.py
+++ b/solution.py
@@ -21,8 +21,8 @@
     "direct": (8, 10, 3, 12, 15),
     "c1": (4,),
     "b0": (6, 13),
-    "c0": (9, 0, 2, 14),
-    "e0": (5, 7, 11, 1),
+    "c0": (9, 0, 2),
+    "e0": (5, 7, 11, 1, 14),
 }
 BETWEEN = {
     4: (("long", (0, 0)), ("cross", (4, 5))),
@@ -50,9 +50,9 @@
 
 
 def kernel(
-    v_hbm, ws_hbm, bs_ref, wt_hbm, bt_ref, o_hbm,
-    vbuf, wraw, traw, wmat, tmat, act, even, prev, obuf, za, zb, longbuf, crossbuf,
-    load_sem, halo_send, halo_recv, send_sem, prev_recv, long_recv, long_send, cross_recv, cross_send, out_sem,
+    v_hbm, ws_hbm, bs_ref, wt_hbm, bt_ref, o_ref,
+    vbuf, wraw, traw, wmat, tmat, act, even, prev, za, zb, longbuf, crossbuf,
+    load_sem, halo_send, halo_recv, send_sem, prev_recv, long_recv, long_send, cross_recv, cross_send,
 ):
     rows, channels, width = act.shape
     groups = channels // GROUP
@@ -282,8 +282,7 @@
         rhs = stacked([[ref[h] for ref in (prev, even, act)] for h in pair])
         total = jnp.dot(tmat[...], rhs, preferred_element_type=F32).astype(BF16)
         for k, h in enumerate(pair):
-            obuf[h] = total[:, k * width : (k + 1) * width]
-            pltpu.make_async_copy(obuf.at[h], o_hbm.at[h], out_sem.at[h]).start()
+            o_ref[h] = total[:, k * width : (k + 1) * width]
 
     finish(taps(*STEPS[0]), act, STEPS[0][1])
     first_sends(STEPS[0][1])
@@ -364,16 +363,13 @@
             def _(name=name, h=h):
                 cross_second(name, h).wait_send()
 
-    for h in range(rows):
-        pltpu.make_async_copy(obuf.at[h], o_hbm.at[h], out_sem.at[h]).wait()
-
 
 def per_device(video, w_spatial, b_spatial, w_temporal, b_temporal):
     frames, rows, width, channels = video.shape
     dma = pltpu.SemaphoreType.DMA
     out = pl.pallas_call(
         kernel,
-        out_shape=jax.ShapeDtypeStruct((rows, channels, width), BF16),
+        out_shape=pltpu.VMEM((rows, channels, width), BF16),
         in_specs=[
             pl.BlockSpec(memory_space=pl.ANY),
             pl.BlockSpec(memory_space=pl.ANY),
@@ -381,14 +377,13 @@
             pl.BlockSpec(memory_space=pl.ANY),
             pl.BlockSpec(memory_space=pltpu.VMEM),
         ],
-        out_specs=pl.BlockSpec(memory_space=pl.ANY),
+        out_specs=pl.BlockSpec(memory_space=pltpu.VMEM),
         scratch_shapes=[
             pltpu.VMEM((frames, rows + 2, channels, width), BF16),
             pltpu.VMEM(w_spatial.shape, BF16),
             pltpu.VMEM(w_temporal.shape, BF16),
             pltpu.VMEM((channels // GROUP, 3, GROUP, 3 * channels + ONES), BF16),
             pltpu.VMEM((channels, 3 * channels + ONES), BF16),
-            pltpu.VMEM((rows, channels, width), BF16),
             pltpu.VMEM((rows, channels, width), BF16),
             pltpu.VMEM((rows, channels, width), BF16),
             pltpu.VMEM((rows, channels, width), BF16),
@@ -405,7 +400,6 @@
             dma((2, len(LONG))),
             dma((rows,)),
             dma((rows,)),
-            dma((rows,)),
         ],
         compiler_params=pltpu.CompilerParams(
             collective_id=0, has_side_effects=True, vmem_limit_bytes=60 * 1024 * 1024

time: 40.7 us -> 38.4 us (0.943)
  local copies, waits for them, and re-layouts: 2.47 us -> 1.06 us
  Pallas kernels: 38 us -> 37.2 us
    unnamed x1, local copies, waits for them, and re-layouts: 2.47 us -> 1.06 us
    pallas_call x1, Pallas kernels: 38 us -> 37.2 us  [per_device(): pl.pallas_call(kernel, out_shape=pltpu.VMEM((rows, channels, width), BF16...]
where the time goes in v3:
time: 38.4 us; the launch traced here: 38.3 us
  Pallas kernels  37.2 us (97%)
  local copies, waits for them, and re-layouts  1.06 us (3%)
    pallas_call x1, Pallas kernels, per_device(): pl.pallas_call(kernel, out_shape=pltpu.VMEM((rows, channels, width), BF16...  37.2 us
    unnamed x1, local copies, waits for them, and re-layouts  1.06 us

profile of v3, /device:TPU:160, one launch (start us, length us, event | category | flops | bytes accessed | tf_op | source)
XLA Modules:
  0.0 38.3 jit_solution(9003588980457635836)
XLA Ops:
  0.0 37.2 %level.1 = bf16[16,320,128]{2,1,0:T(8,128)(2,1)S(1)} custom-call(bf16[2,16,320,128]{3,2,1,0:T(8,128)(2,1)} %bitcast.5, bf16[3,3,320,320]{3,2,1,0:T(8,128)(2,1)} %ws_hbm.1, f32[320]{0:T(512)} %bs_ref.1, bf16[3,320,320]{2,1,0:T(8,128)(2,1)} %wt_hbm.1, f32[320]{0:T(512)} %bt_ref.1), custom_call_target="tpu_custom_call" | custom-call | tf_op jit(solution)/shard_map/level/pallas_call | solution.py:370
  37.2 1.1 %copy.7 = bf16[1,16,128,320]{2,3,1,0:T(8,128)(2,1)} copy(bf16[1,16,128,320]{2,3,1,0:T(8,128)(2,1)S(1)} %bitcast.4) | data formatting | bytes 2621440
